TPU v7x, 512 devices: a whole 4x8x8 slice. The times are simulated.
512 devices in a mesh: blk: 64 (over y, z_hi, core), req: 8 (over z_lo, x).
Axes of the slice: x: 4, y: 8, z: 8 (z_hi: 4, z_lo: 2; z = z_hi * 2 + z_lo), core: 2. Of those that a mesh axis runs over, the one named last changes fastest.
Arguments:
- tokens: bfloat16 [8192, 1024], P('blk'), may hold values from -6 to 6
- w_qkv: bfloat16 [1024, 3, 1024], P(None, None, 'req'), may hold values from -0.1875 to 0.1875
- w_out: bfloat16 [1024, 1024], P('req'), may hold values from -0.75 to 0.75
- k_pages: bfloat16 [1280, 128, 1024], P('blk', None, 'req'), may hold values from -512 to 512
- v_pages: bfloat16 [1280, 128, 1024], P('blk', None, 'req'), may hold values from -18 to 18
- page_table: int32 [320, 4], P('blk'), may hold values from 0 to 19, as said below
- cache_lens: int32 [320], P('blk'), may hold values from 1 to 512, as said below
- norm1_gain: float32 [1024], replicated, may hold values from 0.5 to 1.5
- norm1_shift: float32 [1024], replicated, may hold values from -3 to 3
- w_up: bfloat16 [1024, 4096], P(None, 'blk'), may hold values from -0.1875 to 0.1875
- w_down: bfloat16 [4096, 1024], P('blk'), may hold values from -0.1875 to 0.1875
- norm2_gain: float32 [1024], replicated, may hold values from 0.5 to 1.5
- norm2_shift: float32 [1024], replicated, may hold values from -3 to 3
Outputs:
- layer_out: bfloat16 [8192, 1024], P(('blk', 'req'))
Inputs may be any that keep to these rules, and one draw needn't show every extreme that they name: `page_table`: the 5 rows of one request group name every page of that group's pool exactly once. `cache_lens`: every request group has at least one request whose cache is full.
All inputs are finite; a program needn't handle non-finite values.
Results may differ from a plain program's by a relative error of at most 0.02.
Values may be sent and summed in bfloat16 or wider, within the bound.
A program may use at most 64 MiB of HBM per device.

v0:
```python
import jax
import jax.numpy as jnp
from jax import lax
from jax.sharding import PartitionSpec as P

HD = 64


epsilon = 1e-05
masked_score = -1e30


def layer_norm(values, gain_vec, shift_vec):
    center = values - jnp.mean(values, axis=-1, keepdims=True)
    spread = jnp.mean(center * center, axis=-1, keepdims=True)
    return center * lax.rsqrt(spread + epsilon) * gain_vec + shift_vec


def attend(queries, key_new, value_new, key_pool, value_pool, page_map, lengths):
    requests = page_map.shape[0]
    stretch_len = queries.shape[0] - (requests - 1)
    head_count = key_pool.shape[2]
    head_size = key_pool.shape[3]
    key_seq = key_pool[page_map].reshape(requests, -1, head_count, head_size)
    value_seq = value_pool[page_map].reshape(requests, -1, head_count, head_size)
    scale_factor = head_size ** (-0.5)
    key_span = key_seq.shape[1]
    positions = jnp.arange(key_span)
    prompt_query = queries[:stretch_len]
    cache_scores = (
        jnp.einsum("chd,shd->hcs", prompt_query, key_seq[0], preferred_element_type=jnp.float32)
        * scale_factor
    )
    cache_scores = jnp.where(positions[None, None, :] < lengths[0], cache_scores, masked_score)
    stretch_scores = (
        jnp.einsum(
            "chd,jhd->hcj", prompt_query, key_new[:stretch_len], preferred_element_type=jnp.float32
        )
        * scale_factor
    )
    causal = jnp.arange(stretch_len)[:, None] >= jnp.arange(stretch_len)[None, :]
    stretch_scores = jnp.where(causal[None], stretch_scores, masked_score)
    top_score = jnp.maximum(
        jnp.max(cache_scores, -1, keepdims=True), jnp.max(stretch_scores, -1, keepdims=True)
    )
    cache_exp = jnp.exp(cache_scores - top_score)
    stretch_exp = jnp.exp(stretch_scores - top_score)
    exp_total = jnp.sum(cache_exp, -1, keepdims=True) + jnp.sum(stretch_exp, -1, keepdims=True)
    cache_weight = (cache_exp / exp_total).astype(jnp.bfloat16)
    stretch_weight = (stretch_exp / exp_total).astype(jnp.bfloat16)
    prompt_out = jnp.einsum(
        "hcs,shd->chd", cache_weight, value_seq[0], preferred_element_type=jnp.float32
    )
    prompt_out = prompt_out + jnp.einsum(
        "hcj,jhd->chd", stretch_weight, value_new[:stretch_len], preferred_element_type=jnp.float32
    )
    step_query = queries[stretch_len:]
    step_scores = (
        jnp.einsum("rhd,rshd->rhs", step_query, key_seq[1:], preferred_element_type=jnp.float32)
        * scale_factor
    )
    step_scores = jnp.where(
        positions[None, None, :] < lengths[1:, None, None], step_scores, masked_score
    )
    self_score = (
        jnp.einsum(
            "rhd,rhd->rh", step_query, key_new[stretch_len:], preferred_element_type=jnp.float32
        )[..., None]
        * scale_factor
    )
    step_top = jnp.maximum(jnp.max(step_scores, -1, keepdims=True), self_score)
    step_exp = jnp.exp(step_scores - step_top)
    self_exp = jnp.exp(self_score - step_top)
    step_total = jnp.sum(step_exp, -1, keepdims=True) + self_exp
    step_weight = (step_exp / step_total).astype(jnp.bfloat16)
    self_weight = (self_exp / step_total).astype(jnp.bfloat16)
    step_out = jnp.einsum(
        "rhs,rshd->rhd", step_weight, value_seq[1:], preferred_element_type=jnp.float32
    )
    step_out = step_out + self_weight.astype(jnp.float32) * value_new[stretch_len:].astype(
        jnp.float32
    )
    merged = jnp.concatenate([prompt_out, step_out], axis=0)
    return merged.astype(jnp.bfloat16).reshape(queries.shape[0], head_count * head_size)


def on_device(
    tokens,
    w_qkv,
    w_out,
    k_pages,
    v_pages,
    page_table,
    cache_lens,
    norm1_gain,
    norm1_shift,
    w_up,
    w_down,
    norm2_gain,
    norm2_shift,
):
    tok_rows, model_width = tokens.shape
    head_cols = w_qkv.shape[2]
    head_count = head_cols // HD
    projected = jnp.dot(
        tokens, w_qkv.reshape(model_width, 3 * head_cols), preferred_element_type=jnp.float32
    ).astype(jnp.bfloat16)
    projected = projected.reshape(tok_rows, 3, head_count, HD)
    pool_pages = k_pages.shape[0]
    key_pool = k_pages.reshape(pool_pages, k_pages.shape[1], head_count, HD)
    value_pool = v_pages.reshape(pool_pages, v_pages.shape[1], head_count, HD)
    attended = attend(
        projected[:, 0],
        projected[:, 1],
        projected[:, 2],
        key_pool,
        value_pool,
        page_table,
        cache_lens,
    )
    partial_out = jnp.dot(attended, w_out, preferred_element_type=jnp.float32)
    own_rows = tok_rows // lax.axis_size("req")
    row_first = lax.axis_index("req") * own_rows
    summed = lax.psum(partial_out.astype(jnp.bfloat16), "req").astype(jnp.float32)
    head_mixed = lax.dynamic_slice_in_dim(summed, row_first, own_rows, 0)
    residual = lax.dynamic_slice_in_dim(tokens, row_first, own_rows, 0).astype(jnp.float32)
    normed = layer_norm(residual + head_mixed, norm1_gain, norm1_shift).astype(jnp.bfloat16)
    hidden = jax.nn.gelu(
        jnp.dot(
            lax.all_gather(normed, "blk", axis=0, tiled=True),
            w_up,
            preferred_element_type=jnp.float32,
        ),
        approximate=False,
    ).astype(jnp.bfloat16)
    branch = lax.psum_scatter(
        jnp.dot(hidden, w_down, preferred_element_type=jnp.float32),
        "blk",
        scatter_dimension=0,
        tiled=True,
    )
    return layer_norm(normed.astype(jnp.float32) + branch, norm2_gain, norm2_shift).astype(
        jnp.bfloat16
    )


def solution(mesh):
    return jax.shard_map(
        on_device,
        mesh=mesh,
        in_specs=(
            P("blk", None),
            P(None, None, "req"),
            P("req", None),
            P("blk", None, "req"),
            P("blk", None, "req"),
            P("blk", None),
            P("blk"),
            P(),
            P(),
            P(None, "blk"),
            P("blk", None),
            P(),
            P(),
        ),
        out_specs=P(("blk", "req"), None),
        check_vma=False,
    )
```

profile of v0, /device:TPU:1, one launch (start us, length us, event | category | flops | bytes accessed | tf_op | source)
XLA Modules:
  0.0 361.8 jit_solution(5662125291629240805)
XLA Ops:
  6.6 1.5 copy.45
  8.1 1.3 convolution_convert_fusion.1
  9.4 0.1 copy.46
  10.1 0.3 copy.47
  10.5 0.7 gather_fusion.1
  11.2 0.3 copy.50
  11.6 0.2 slice.82
  11.8 0.5 copy-done.3
  12.2 0.3 copy.42
  12.6 0.7 gather_fusion
  13.3 0.3 copy.51
  13.7 0.2 slice.86
  13.9 0.3 fusion.105
  14.3 0.2 fusion.5
  14.7 0.2 fusion.69
  14.9 0.2 fusion.3
  15.2 0.1 copy.61
  15.3 0.2 fusion.106
  15.6 0.2 fusion.7
  15.9 0.3 fusion.18
  16.2 0.2 fusion.2
  16.5 1.0 convolution_convert_fusion
  17.6 85.9 %all-reduce.2.cloned.1.call-done = bf16[128,1024]{1,0:T(8,128)(2,1)} async-done(((bf16[128,1024]{1,0:T(8,128)(2,1)}), bf16[128,1024]{1,0:T(8,128)(2,1)}) %all-reduce.2.cloned.1.call-update) | async-done | bytes 262160 | tf_op jit(solution)/shard_map/psum | solution.py:124
  103.5 0.9 fusion.62
  104.4 1.0 multiply_reduce_fusion.1
  105.4 1.5 add_convert_fusion.1
  107.0 89.8 %all-gather.2.cloned.1.call-done = bf16[1024,1024]{1,0:T(8,128)(2,1)} async-done(((bf16[16,1024]{1,0:T(8,128)(2,1)}), bf16[1024,1024]{1,0:T(8,128)(2,1)}) %all-gather.2.cloned.1.call-update) | async-done | bytes 2097168 | tf_op jit(solution)/shard_map/all_gather | solution.py:130
  196.7 5.3 %fusion.19 = f32[1024,1024]{1,0:T(8,128)} fusion(bf16[64,1024]{1,0:T(8,128)(2,1)S(1)} %copy-done.9, bf16[1024,1024]{1,0:T(8,128)(2,1)} %all-gather.2.cloned.1.call-done, bf16[1024,64]{0,1:T(8,128)(2,1)S(1)} %copy-done.10), kind=kOutput, calls=%fused_computation.37 | convolution fusion | flops 272695296 | bytes 6553600 | tf_op jit(solution)/shard_map/dot_general | solution.py:137
  202.1 149.6 %reduce-scatter.2.cloned.1.call-done = f32[16,1024]{1,0:T(8,128)} async-done(((f32[1024,1024]{1,0:T(8,128)}), f32[16,1024]{1,0:T(8,128)}) %reduce-scatter.2.cloned.1.call-update) | async-done | bytes 65552 | tf_op jit(solution)/shard_map/reduce_scatter | solution.py:136
  351.7 1.0 fusion.66
  352.7 1.0 multiply_reduce_fusion
  353.7 1.5 add_convert_fusion
  (54 shorter events, 1.4 us)
Async XLA Ops:
  6.5 9.9 %copy-start = (bf16[128,1024]{1,0:T(8,128)(2,1)S(1)}, bf16[128,1024]{1,0:T(8,128)(2,1)}, u32[]{:S(2)}) copy-start(bf16[128,1024]{1,0:T(8,128)(2,1)} %param.15) | copy-start | bytes 786436
  6.5 3.2 copy-start.11
  6.5 3.4 copy-start.8
  6.5 3.6 copy-start.2
  6.5 97.0 %all-reduce.2.cloned.1.call-start = ((), (), s32[]{:S(2)}) async-start(), calls=%async_computation.1 | async-start | bytes 524288 | tf_op jit(solution)/shard_map/psum | solution.py:124
  11.2 1.1 copy-start.3
  15.8 89.5 %copy-start.6 = (f32[1024]{0:T(1024)S(1)}, f32[1024]{0:T(1024)}, u32[]{:S(2)}) copy-start(f32[1024]{0:T(1024)} %param.21) | copy-start | bytes 12292
  15.8 89.5 %copy-start.7 = (f32[1024]{0:T(1024)S(1)}, f32[1024]{0:T(1024)}, u32[]{:S(2)}) copy-start(f32[1024]{0:T(1024)} %param.20) | copy-start | bytes 12292
  15.9 180.9 %copy-start.9 = (bf16[64,1024]{1,0:T(8,128)(2,1)S(1)}, bf16[64,1024]{1,0:T(8,128)(2,1)}, u32[]{:S(2)}) copy-start(bf16[64,1024]{1,0:T(8,128)(2,1)} %param.23) | copy-start | bytes 393220
  15.9 180.9 %copy-start.10 = (bf16[1024,64]{0,1:T(8,128)(2,1)S(1)}, bf16[1024,64]{0,1:T(8,128)(2,1)}, u32[]{:S(2)}) copy-start(bf16[1024,64]{0,1:T(8,128)(2,1)} %param.22) | copy-start | bytes 393220
  17.5 179.2 %all-gather.2.cloned.1.call-start = ((), (), s32[]{:S(2)}) async-start(), calls=%async_computation.2 | async-start | bytes 2129920 | tf_op jit(solution)/shard_map/all_gather | solution.py:130
  106.9 244.8 %reduce-scatter.2.cloned.1.call-start = ((), (), s32[]{:S(2)}) async-start(), calls=%async_computation.3 | async-start | bytes 4259840 | tf_op jit(solution)/shard_map/reduce_scatter | solution.py:136
  202.1 149.6 %copy-start.1 = (bf16[16,1024]{1,0:T(8,128)(2,1)S(1)}, bf16[16,1024]{1,0:T(8,128)(2,1)}, u32[]{:S(2)}) copy-start(bf16[16,1024]{1,0:T(8,128)(2,1)} %add_convert_fusion.1) | copy-start | bytes 98308
  202.1 151.7 %copy-start.4 = (f32[1024]{0:T(1024)S(1)}, f32[1024]{0:T(1024)}, u32[]{:S(2)}) copy-start(f32[1024]{0:T(1024)} %param.25) | copy-start | bytes 12292
  202.1 151.7 %copy-start.5 = (f32[1024]{0:T(1024)S(1)}, f32[1024]{0:T(1024)}, u32[]{:S(2)}) copy-start(f32[1024]{0:T(1024)} %param.24) | copy-start | bytes 12292
Sparse Core Ops, SparseCore 0:
  17.7 85.7 all-reduce.1
  107.0 89.6 all-gather.1
  202.2 149.4 reduce-scatter.1
where the time goes:
time: 366 us; the launch traced here: 362 us
  waiting for transfers between devices  325 us (89%)
  between operations  13.4 us (4%)
  matrix products  9.21 us (3%)
  other arithmetic  7.88 us (2%)
  local copies, waits for them, and re-layouts  5.86 us (2%)
    reduce_scatter x1, waiting for transfers between devices, on_device(): lax.psum_scatter(jnp.dot(hidden, w_down, preferred_element_type=jnp.float...  150 us
    all_gather x1, waiting for transfers between devices, on_device(): lax.all_gather(normed, 'blk', axis=0, tiled=True)  89.8 us
    psum x1, waiting for transfers between devices, on_device(): lax.psum(partial_out.astype(jnp.bfloat16), 'req').astype(jnp.float32)  85.9 us
  transfers between devices with their start and end apart: 3, of which 3 were waited for; matrix products, arithmetic and copies ran while one was open for 0% of the time, Pallas kernels for 0%

commit v1 on v0

--- a/solution.py
+++ b/solution.py
@@ -1,13 +1,15 @@
 import jax
 import jax.numpy as jnp
 from jax import lax
+from jax.experimental import pallas as pl
+from jax.experimental.pallas import tpu as pltpu
 from jax.sharding import PartitionSpec as P
 
 HD = 64
-
-
+MESH = pl.DeviceIdType.MESH
 epsilon = 1e-05
 masked_score = -1e30
+NT = (((1,), (1,)), ((), ()))
 
 
 def layer_norm(values, gain_vec, shift_vec):
@@ -82,6 +84,215 @@
     )
     merged = jnp.concatenate([prompt_out, step_out], axis=0)
     return merged.astype(jnp.bfloat16).reshape(queries.shape[0], head_count * head_size)
+
+
+def tail_kernel(
+    part_ref,
+    tok_ref,
+    g1_ref,
+    s1_ref,
+    pair_ref,
+    g2_ref,
+    s2_ref,
+    out_ref,
+    wts,
+    head_in,
+    rows_in,
+    back_out,
+    back_in,
+    local_sem,
+    o_send,
+    o_recv,
+    i_send,
+    i_recv,
+    c_send,
+    c_recv,
+    h_send,
+    h_recv,
+    y_send,
+    y_recv,
+    b_send,
+    b_recv,
+):
+    blk = lax.axis_index("blk")
+    req = lax.axis_index("req")
+    y = blk // 8
+    k = (blk // 2) % 4
+    core = blk % 2
+    zlo = req // 4
+    x = req % 4
+    step = 2 * zlo - 1
+    outer = (y * 8 + ((k + step + 4) % 4) * 2 + core, (1 - zlo) * 4 + x)
+    inner = (blk, (1 - zlo) * 4 + x)
+    sibling = (blk + 1 - 2 * core, req)
+
+    def across(d):
+        return (blk, (req + d) % 8)
+
+    def along(d):
+        return (((y + d) % 8) * 8 + blk % 8, req)
+
+    barrier = pltpu.get_barrier_semaphore()
+    for peer in [across(d) for d in range(1, 8)] + [along(d) for d in range(1, 8)] + [outer, sibling]:
+        pl.semaphore_signal(barrier, inc=1, device_id=peer, device_id_type=MESH)
+    pl.semaphore_wait(barrier, 16)
+
+    def copy(src, dst, send, recv, peer):
+        return pltpu.make_async_remote_copy(
+            src_ref=src,
+            dst_ref=dst,
+            send_sem=send,
+            recv_sem=recv,
+            device_id=peer,
+            device_id_type=MESH,
+        )
+
+    def slot(dk):
+        return ((k + dk + 8) % 4) * 2 + core
+
+    from_o = [(zlo, slot(step)), (1 - zlo, slot(step)), (zlo, slot(2 * step))]
+    from_i = [(1 - zlo, slot(-step)), (zlo, slot(-step)), (1 - zlo, slot(-2 * step))]
+    own = slot(0)
+
+    def at(c):
+        return wts.at[c[0], c[1]]
+
+    local = pltpu.make_async_copy(pair_ref, wts.at[:, own], local_sem)
+    local.start()
+    head = [
+        copy(
+            part_ref.at[pl.ds(pl.multiple_of(across(d)[1] * 16, 16), 16)],
+            head_in.at[d],
+            h_send.at[d],
+            h_recv.at[d],
+            across(d),
+        )
+        for d in range(1, 8)
+    ]
+    to_o = [
+        copy(pair_ref.at[1 - zlo], wts.at[1 - zlo, own], o_send.at[0], o_recv.at[0], outer),
+        copy(pair_ref.at[zlo], wts.at[zlo, own], o_send.at[1], o_recv.at[1], outer),
+        copy(at(from_i[0]), at(from_i[0]), o_send.at[2], o_recv.at[2], outer),
+    ]
+    to_i = [copy(at(c), at(c), i_send.at[j], i_recv.at[j], inner) for j, c in enumerate(from_o)]
+    to_c = [
+        copy(pair_ref.at[0], wts.at[0, own], c_send.at[0], c_recv.at[0], sibling),
+        copy(pair_ref.at[1], wts.at[1, own], c_send.at[1], c_recv.at[1], sibling),
+    ] + [
+        copy(at(c), at(c), c_send.at[2 + j], c_recv.at[2 + j], sibling)
+        for j, c in enumerate(from_o + from_i)
+    ]
+
+    for c in head:
+        c.start()
+    to_o[0].start()
+    to_o[1].start()
+    to_c[0].start()
+    to_c[1].start()
+
+    def relay_o(j):
+        to_o[j].wait_recv()
+        to_i[j].start()
+        to_c[2 + j].start()
+
+    def relay_i(j):
+        to_i[j].wait_recv()
+        if j == 0:
+            to_o[2].start()
+        to_c[5 + j].start()
+
+    relay_o(0)
+    relay_i(0)
+
+    for c in head:
+        c.wait_recv()
+    mine = pl.ds(pl.multiple_of(req * 16, 16), 16)
+    mixed = part_ref[mine].astype(jnp.float32)
+    for d in range(1, 8):
+        mixed = mixed + head_in[d].astype(jnp.float32)
+    normed = layer_norm(
+        tok_ref[mine].astype(jnp.float32) + mixed, g1_ref[...], s1_ref[...]
+    ).astype(jnp.bfloat16)
+    rows_in[0] = normed
+    send_rows = [
+        copy(rows_in.at[0], rows_in.at[d], y_send.at[d], y_recv.at[d], along(d))
+        for d in (4, 3, 5, 2, 6, 1, 7)
+    ]
+    for c in send_rows:
+        c.start()
+
+    relay_o(1)
+    relay_i(1)
+    relay_o(2)
+    relay_i(2)
+    local.wait()
+    for c in to_c:
+        c.wait_recv()
+    for c in send_rows:
+        c.wait_recv()
+
+    rows = rows_in[...].reshape(128, 1024)
+    up = wts[0].reshape(512, 1024)
+    pre = lax.dot_general(rows, up, NT, preferred_element_type=jnp.float32)
+    hidden = (0.5 * pre * (1.0 + lax.erf(pre * (2.0**-0.5)))).astype(jnp.bfloat16)
+    down = wts[1].reshape(512, 1024)
+    total = jnp.dot(hidden, down, preferred_element_type=jnp.float32)
+    back_out[...] = total[16:].astype(jnp.bfloat16).reshape(7, 16, 1024)
+    send_back = [
+        copy(back_out.at[d - 1], back_in.at[d], b_send.at[d], b_recv.at[d], along(8 - d))
+        for d in (4, 3, 5, 2, 6, 1, 7)
+    ]
+    for c in send_back:
+        c.start()
+    branch = total[:16]
+    for c in send_back:
+        c.wait_recv()
+    for d in range(1, 8):
+        branch = branch + back_in[d].astype(jnp.float32)
+    out_ref[...] = layer_norm(
+        normed.astype(jnp.float32) + branch, g2_ref[...], s2_ref[...]
+    ).astype(jnp.bfloat16)
+    for c in head + to_o + to_i + to_c + send_rows + send_back:
+        c.wait_send()
+
+
+def tail(partial_out, tokens, norm1_gain, norm1_shift, pair, norm2_gain, norm2_shift):
+    dma = pltpu.SemaphoreType.DMA
+    return pl.pallas_call(
+        tail_kernel,
+        out_shape=jax.ShapeDtypeStruct((16, 1024), jnp.bfloat16),
+        in_specs=[pl.BlockSpec(memory_space=pltpu.VMEM)] * 7,
+        out_specs=pl.BlockSpec(memory_space=pltpu.VMEM),
+        scratch_shapes=[
+            pltpu.VMEM((2, 8, 64, 1024), jnp.bfloat16),
+            pltpu.VMEM((8, 16, 1024), jnp.bfloat16),
+            pltpu.VMEM((8, 16, 1024), jnp.bfloat16),
+            pltpu.VMEM((7, 16, 1024), jnp.bfloat16),
+            pltpu.VMEM((8, 16, 1024), jnp.bfloat16),
+            dma,
+            dma((3,)),
+            dma((3,)),
+            dma((3,)),
+            dma((3,)),
+            dma((8,)),
+            dma((8,)),
+            dma((8,)),
+            dma((8,)),
+            dma((8,)),
+            dma((8,)),
+            dma((8,)),
+            dma((8,)),
+        ],
+        compiler_params=pltpu.CompilerParams(collective_id=0, has_side_effects=True),
+    )(
+        partial_out,
+        tokens,
+        norm1_gain.reshape(1, 1024),
+        norm1_shift.reshape(1, 1024),
+        pair,
+        norm2_gain.reshape(1, 1024),
+        norm2_shift.reshape(1, 1024),
+    )
 
 
 def on_device(
@@ -102,6 +313,7 @@
     tok_rows, model_width = tokens.shape
     head_cols = w_qkv.shape[2]
     head_count = head_cols // HD
+    pair = jnp.stack([w_up.T, w_down])
     projected = jnp.dot(
         tokens, w_qkv.reshape(model_width, 3 * head_cols), preferred_element_type=jnp.float32
     ).astype(jnp.bfloat16)
@@ -119,28 +331,14 @@
         cache_lens,
     )
     partial_out = jnp.dot(attended, w_out, preferred_element_type=jnp.float32)
-    own_rows = tok_rows // lax.axis_size("req")
-    row_first = lax.axis_index("req") * own_rows
-    summed = lax.psum(partial_out.astype(jnp.bfloat16), "req").astype(jnp.float32)
-    head_mixed = lax.dynamic_slice_in_dim(summed, row_first, own_rows, 0)
-    residual = lax.dynamic_slice_in_dim(tokens, row_first, own_rows, 0).astype(jnp.float32)
-    normed = layer_norm(residual + head_mixed, norm1_gain, norm1_shift).astype(jnp.bfloat16)
-    hidden = jax.nn.gelu(
-        jnp.dot(
-            lax.all_gather(normed, "blk", axis=0, tiled=True),
-            w_up,
-            preferred_element_type=jnp.float32,
-        ),
-        approximate=False,
-    ).astype(jnp.bfloat16)
-    branch = lax.psum_scatter(
-        jnp.dot(hidden, w_down, preferred_element_type=jnp.float32),
-        "blk",
-        scatter_dimension=0,
-        tiled=True,
-    )
-    return layer_norm(normed.astype(jnp.float32) + branch, norm2_gain, norm2_shift).astype(
-        jnp.bfloat16
+    return tail(
+        partial_out.astype(jnp.bfloat16),
+        tokens,
+        norm1_gain,
+        norm1_shift,
+        pair,
+        norm2_gain,
+        norm2_shift,
     )
 
 

time: 366 us -> 57.6 us (0.16); the launches traced: 362 us -> 57.3 us
  waiting for transfers between devices: 325 us -> 0 us
  Pallas kernels: 0 us -> 45.1 us
  between operations: 13.4 us -> 0.26 us
  matrix products: 9.21 us -> 2.92 us
  other arithmetic: 7.88 us -> 1.7 us
    reduce_scatter x1 -> x0, waiting for transfers between devices: 150 us -> none  [on_device(): lax.psum_scatter(jnp.dot(hidden, w_down, preferred_element_type=jnp.float...]
    all_gather x1 -> x0, waiting for transfers between devices: 89.8 us -> none  [on_device(): lax.all_gather(normed, 'blk', axis=0, tiled=True)]
    psum x1 -> x0, waiting for transfers between devices: 85.9 us -> none  [on_device(): lax.psum(partial_out.astype(jnp.bfloat16), 'req').astype(jnp.float32)]
    pallas_call x0 -> x1, Pallas kernels: none -> 45.1 us  [tail(): pl.pallas_call(tail_kernel, out_shape=jax.ShapeDtypeStruct((16, 1024), jn...]
    dot_general x1 -> x0, matrix products: 5.32 us -> none  [on_device(): jnp.dot(hidden, w_down, preferred_element_type=jnp.float32)]
    reduce_sum x4 -> x0, other arithmetic: 3.85 us -> none  [the longest x2 2 us: layer_norm(): spread = jnp.mean(center * center, axis=-1, keepdims=True)]
  transfers between devices with their start and end apart: 3 -> 0, of which waited for: 3 -> 0; matrix products, arithmetic and copies ran while one was open for 0% -> 0% of each run, Pallas kernels for 0% -> 0%
where the time goes in v1:
time: 57.6 us; the launch traced here: 57.3 us
  Pallas kernels  45.1 us (78%)
  local copies, waits for them, and re-layouts  7.28 us (13%)
  matrix products  2.92 us (5%)
  other arithmetic  1.7 us (3%)
    pallas_call x1, Pallas kernels, tail(): pl.pallas_call(tail_kernel, out_shape=jax.ShapeDtypeStruct((16, 1024), jn...  45.1 us
    unnamed x20, local copies, waits for them, and re-layouts  4.08 us

profile of v1, /device:TPU:1, one launch (start us, length us, event | category | flops | bytes accessed | tf_op | source)
XLA Modules:
  0.0 57.3 jit_solution(8450381850529673906)
XLA Ops:
  0.0 1.5 %copy.45 = bf16[1024,3,128]{0,2,1:T(8,128)(2,1)S(1)} copy(bf16[1024,3,128]{2,0,1:T(8,128)(2,1)} %param.14) | data formatting | bytes 1572864 | tf_op args[1]
  1.5 0.4 convolution_convert_fusion.1
  1.9 0.1 copy.46
  2.0 0.1 copy-done.6
  2.2 0.1 copy.43
  2.3 0.2 copy-done.2
  2.6 0.3 copy.47
  2.9 0.7 %gather_fusion.1 = bf16[20,128,2,64]{1,3,2,0:T(8,128)(2,1)S(1)} fusion(bf16[20,128,2,64]{1,3,2,0:T(8,128)(2,1)S(1)} %bitcast.90, s32[1024]{0:T(1024)S(1)} %pad_clamp_fusion), kind=kCustom, calls=%fused_computation.1 | custom fusion | bytes 1310800 | tf_op jit(solution)/shard_map/gather | solution.py:26
  3.7 0.3 fusion.30
  4.0 0.2 fusion.31
  4.3 0.2 fusion.7
  4.6 0.2 copy-done.3
  4.8 0.3 copy.42
  5.1 0.7 %gather_fusion = bf16[20,128,2,64]{1,3,2,0:T(8,128)(2,1)S(1)} fusion(bf16[20,128,2,64]{1,3,2,0:T(8,128)(2,1)S(1)} %bitcast.89, s32[1024]{0:T(1024)S(1)} %pad_clamp_fusion), kind=kCustom, calls=%fused_computation | custom fusion | bytes 1310800 | tf_op jit(solution)/shard_map/gather | solution.py:27
  5.8 0.3 fusion.8
  6.1 0.2 fusion.2
  6.4 0.1 copy.53
  6.5 0.3 copy.50
  6.9 0.2 slice.82
  7.1 0.2 fusion.5
  7.4 0.1 fusion.26
  7.5 0.1 fusion.16
  7.6 0.2 fusion.24
  7.8 0.1 fusion.25
  8.0 0.3 copy.51
  8.3 0.2 slice.86
  8.6 0.2 fusion.3
  8.8 0.1 copy.61
  9.0 1.0 %convolution_convert_fusion.part_ref = bf16[128,1024]{1,0:T(8,128)(2,1)} fusion(bf16[128,1024]{1,0:T(8,128)(2,1)S(1)} %copy-done, bf16[4,128]{0,1:T(8,128)(2,1)S(1)} %bitcast.98, bf16[124,128]{0,1:T(8,128)(2,1)S(1)} %bitcast.101), kind=kOutput, calls=%fused_computation.4 | convolution fusion | flops 33751040 | bytes 557056 | tf_op jit(solution)/shard_map/dot_general | solution.py:333
  10.1 0.7 %pad_maximum_fusion.pair_ref = bf16[2,64,1024]{2,1,0:T(8,128)(2,1)} fusion(bf16[1,64,1024]{2,1,0:T(8,128)(2,1)S(1)} %bitcast.99, bf16[1,64,1024]{2,1,0:T(8,128)(2,1)S(1)} %bitcast.100), kind=kLoop, calls=%fused_computation.17 | loop fusion | flops 131072 | bytes 524288 | tf_op jit(solution)/shard_map/stack | solution.py:316
  10.8 45.1 %shard_map.127 = bf16[16,1024]{1,0:T(8,128)(2,1)} custom-call(bf16[128,1024]{1,0:T(8,128)(2,1)} %convolution_convert_fusion.part_ref, bf16[128,1024]{1,0:T(8,128)(2,1)} %tok_ref.1, f32[1,1024]{1,0:T(1,128)} %bitcast.102, f32[1,1024]{1,0:T(1,128)} %bitcast.103, bf16[2,64,1024]{2,1,0:T(8,128)(2,1)} %pad_maximum_fusion.pair_ref, f32[1,1024]{1,0:T(1,128)} %bitcast.104, ...), custom_call_target="tpu_custom_call" | custom-call | tf_op jit(solution)/shard_map/pallas_call | solution.py:261
  55.9 1.4 %copy.89 = bf16[16,1024]{1,0:T(8,128)(2,1)} copy(bf16[16,1024]{1,0:T(8,128)(2,1)} %shard_map.127) | data formatting | bytes 65536
  (29 shorter events, 0.7 us)
Async XLA Ops:
  0.0 9.0 %copy-start = (bf16[128,1024]{1,0:T(8,128)(2,1)S(1)}, bf16[128,1024]{1,0:T(8,128)(2,1)}, u32[]{:S(2)}) copy-start(bf16[128,1024]{1,0:T(8,128)(2,1)} %param.15) | copy-start | bytes 786436
  0.0 1.5 %copy-start.1 = (bf16[128,1024]{1,0:T(8,128)(2,1)S(1)}, bf16[128,1024]{1,0:T(8,128)(2,1)}, u32[]{:S(2)}) copy-start(bf16[128,1024]{1,0:T(8,128)(2,1)} %tok_ref.1) | copy-start | bytes 786436
  1.5 0.7 %copy-start.6 = (s32[5,4]{0,1:T(4,128)S(1)}, s32[5,4]{0,1:T(4,128)}, u32[]{:S(2)}) copy-start(s32[5,4]{0,1:T(4,128)} %param.18) | copy-start | bytes 244
  1.5 1.1 %copy-start.2 = (bf16[20,128,128]{2,1,0:T(8,128)(2,1)S(1)}, bf16[20,128,128]{2,1,0:T(8,128)(2,1)}, u32[]{:S(2)}) copy-start(bf16[20,128,128]{2,1,0:T(8,128)(2,1)} %param.16) | copy-start | bytes 1966084
  2.9 0.7 %copy-start.7 = (s32[5]{0:T(128)S(1)}, s32[5]{0:T(128)}, u32[]{:S(2)}) copy-start(s32[5]{0:T(128)} %param.19) | copy-start | bytes 64
  3.7 1.1 %copy-start.3 = (bf16[20,128,128]{2,1,0:T(8,128)(2,1)S(1)}, bf16[20,128,128]{2,1,0:T(8,128)(2,1)}, u32[]{:S(2)}) copy-start(bf16[20,128,128]{2,1,0:T(8,128)(2,1)} %param.17) | copy-start | bytes 1966084
  8.5 1.5 %copy-start.4 = (bf16[64,1024]{1,0:T(8,128)(2,1)S(1)}, bf16[64,1024]{1,0:T(8,128)(2,1)}, u32[]{:S(2)}) copy-start(bf16[64,1024]{1,0:T(8,128)(2,1)} %param.23) | copy-start | bytes 393220
  8.5 1.5 %copy-start.5 = (bf16[1024,64]{0,1:T(8,128)(2,1)S(1)}, bf16[1024,64]{0,1:T(8,128)(2,1)}, u32[]{:S(2)}) copy-start(bf16[1024,64]{0,1:T(8,128)(2,1)} %param.22) | copy-start | bytes 393220

commit v2 on v1

v2 whole, which is shorter than its diff:
```python
import jax
import jax.numpy as jnp
from jax import lax
from jax.experimental import pallas as pl
from jax.experimental.pallas import tpu as pltpu
from jax.sharding import PartitionSpec as P

HD = 64
PROMPT = 124
MESH = pl.DeviceIdType.MESH
epsilon = 1e-05
masked_score = -1e30
NT = (((1,), (1,)), ((), ()))


def layer_norm(values, gain_vec, shift_vec):
    center = values - jnp.mean(values, axis=-1, keepdims=True)
    spread = jnp.mean(center * center, axis=-1, keepdims=True)
    return center * lax.rsqrt(spread + epsilon) * gain_vec + shift_vec


def attention(proj, k_ref, v_ref, table_ref, lens_ref):
    query = (proj[:, :128] * 0.125).astype(jnp.bfloat16)
    key_new = proj[:, 128:256]
    value_new = proj[:, 256:]

    def heads(rows):
        low = lax.broadcasted_iota(jnp.int32, rows.shape, 1) < HD
        zero = jnp.zeros_like(rows)
        return jnp.concatenate([jnp.where(low, rows, zero), jnp.where(low, zero, rows)], axis=0)

    def attend(rows, first, keys, values, valid):
        count = rows.shape[0]
        both = heads(rows)
        old = lax.dot_general(both, keys, NT, preferred_element_type=jnp.float32)
        old = jnp.where(valid, old, masked_score)
        new = lax.dot_general(both, key_new, NT, preferred_element_type=jnp.float32)
        token = lax.broadcasted_iota(jnp.int32, new.shape, 0) % count + first
        other = lax.broadcasted_iota(jnp.int32, new.shape, 1)
        seen = (other == token) | ((other < token) & (token < PROMPT))
        new = jnp.where(seen, new, masked_score)
        top = jnp.maximum(jnp.max(old, -1, keepdims=True), jnp.max(new, -1, keepdims=True))
        old = jnp.exp(old - top)
        new = jnp.exp(new - top)
        total = jnp.sum(old, -1, keepdims=True) + jnp.sum(new, -1, keepdims=True)
        mixed = jnp.dot(old.astype(jnp.bfloat16), values, preferred_element_type=jnp.float32)
        mixed = mixed + jnp.dot(
            new.astype(jnp.bfloat16), value_new, preferred_element_type=jnp.float32
        )
        mixed = mixed / total
        low = lax.broadcasted_iota(jnp.int32, (count, 128), 1) < HD
        return jnp.where(low, mixed[:count], mixed[count:])

    def cached(ref, request):
        return [ref[table_ref[request, p]] for p in range(4)]

    column = lax.broadcasted_iota(jnp.int32, (1, 512), 1)
    prompt = attend(
        query,
        0,
        jnp.concatenate(cached(k_ref, 0), axis=0),
        jnp.concatenate(cached(v_ref, 0), axis=0),
        column < lens_ref[0],
    )
    column = lax.broadcasted_iota(jnp.int32, (32, 2048), 1)
    row = lax.broadcasted_iota(jnp.int32, (32, 2048), 0) % 16 - 12
    valid = jnp.zeros((32, 2048), jnp.bool_)
    for i in range(4):
        position = column - 512 * i
        valid = valid | ((row == i) & (position >= 0) & (position < lens_ref[1 + i]) & (position < 512))
    decode = attend(
        query[112:],
        112,
        jnp.concatenate([page for i in range(4) for page in cached(k_ref, 1 + i)], axis=0),
        jnp.concatenate([page for i in range(4) for page in cached(v_ref, 1 + i)], axis=0),
        valid,
    )
    last = lax.broadcasted_iota(jnp.int32, (16, 128), 0) >= 12
    return jnp.concatenate(
        [prompt[:112], jnp.where(last, decode, prompt[112:])], axis=0
    ).astype(jnp.bfloat16)


def layer_kernel(
    tok_ref,
    wqkv_ref,
    wout_ref,
    k_ref,
    v_ref,
    table_ref,
    lens_ref,
    g1_ref,
    s1_ref,
    pair_ref,
    g2_ref,
    s2_ref,
    out_ref,
    part_ref,
    wts,
    head_in,
    rows_in,
    back_out,
    back_in,
    local_sem,
    o_send,
    o_recv,
    i_send,
    i_recv,
    c_send,
    c_recv,
    h_send,
    h_recv,
    y_send,
    y_recv,
    b_send,
    b_recv,
):
    blk = lax.axis_index("blk")
    req = lax.axis_index("req")
    y = blk // 8
    k = (blk // 2) % 4
    core = blk % 2
    zlo = req // 4
    x = req % 4
    step = 2 * zlo - 1
    outer = (y * 8 + ((k + step + 4) % 4) * 2 + core, (1 - zlo) * 4 + x)
    inner = (blk, (1 - zlo) * 4 + x)
    sibling = (blk + 1 - 2 * core, req)

    def across(d):
        return (blk, (req + d) % 8)

    def along(d):
        return (((y + d) % 8) * 8 + blk % 8, req)

    barrier = pltpu.get_barrier_semaphore()
    for peer in [across(d) for d in range(1, 8)] + [along(d) for d in range(1, 8)] + [outer, sibling]:
        pl.semaphore_signal(barrier, inc=1, device_id=peer, device_id_type=MESH)
    proj = jnp.dot(
        tok_ref[...], wqkv_ref[...], preferred_element_type=jnp.float32
    ).astype(jnp.bfloat16)
    attended = attention(proj, k_ref, v_ref, table_ref, lens_ref)
    part_ref[...] = jnp.dot(
        attended, wout_ref[...], preferred_element_type=jnp.float32
    ).astype(jnp.bfloat16)
    pl.semaphore_wait(barrier, 16)

    def copy(src, dst, send, recv, peer):
        return pltpu.make_async_remote_copy(
            src_ref=src,
            dst_ref=dst,
            send_sem=send,
            recv_sem=recv,
            device_id=peer,
            device_id_type=MESH,
        )

    def slot(dk):
        return ((k + dk + 8) % 4) * 2 + core

    from_o = [(zlo, slot(step)), (1 - zlo, slot(step)), (zlo, slot(2 * step))]
    from_i = [(1 - zlo, slot(-step)), (zlo, slot(-step)), (1 - zlo, slot(-2 * step))]
    own = slot(0)

    def at(c):
        return wts.at[c[0], c[1]]

    local = pltpu.make_async_copy(pair_ref, wts.at[:, own], local_sem)
    local.start()
    head = [
        copy(
            part_ref.at[pl.ds(pl.multiple_of(across(d)[1] * 16, 16), 16)],
            head_in.at[d],
            h_send.at[d],
            h_recv.at[d],
            across(d),
        )
        for d in range(1, 8)
    ]
    to_o = [
        copy(pair_ref.at[1 - zlo], wts.at[1 - zlo, own], o_send.at[0], o_recv.at[0], outer),
        copy(pair_ref.at[zlo], wts.at[zlo, own], o_send.at[1], o_recv.at[1], outer),
        copy(at(from_i[0]), at(from_i[0]), o_send.at[2], o_recv.at[2], outer),
    ]
    to_i = [copy(at(c), at(c), i_send.at[j], i_recv.at[j], inner) for j, c in enumerate(from_o)]
    to_c = [
        copy(pair_ref.at[0], wts.at[0, own], c_send.at[0], c_recv.at[0], sibling),
        copy(pair_ref.at[1], wts.at[1, own], c_send.at[1], c_recv.at[1], sibling),
    ] + [
        copy(at(c), at(c), c_send.at[2 + j], c_recv.at[2 + j], sibling)
        for j, c in enumerate(from_o + from_i)
    ]

    for c in head:
        c.start()
    to_o[0].start()
    to_o[1].start()
    to_c[0].start()
    to_c[1].start()

    def relay_o(j):
        to_o[j].wait_recv()
        to_i[j].start()
        to_c[2 + j].start()

    def relay_i(j):
        to_i[j].wait_recv()
        if j == 0:
            to_o[2].start()
        to_c[5 + j].start()

    relay_o(0)
    relay_i(0)

    for c in head:
        c.wait_recv()
    mine = pl.ds(pl.multiple_of(req * 16, 16), 16)
    mixed = part_ref[mine].astype(jnp.float32)
    for d in range(1, 8):
        mixed = mixed + head_in[d].astype(jnp.float32)
    normed = layer_norm(
        tok_ref[mine].astype(jnp.float32) + mixed, g1_ref[...], s1_ref[...]
    ).astype(jnp.bfloat16)
    rows_in[0] = normed
    send_rows = [
        copy(rows_in.at[0], rows_in.at[d], y_send.at[d], y_recv.at[d], along(d))
        for d in (4, 3, 5, 2, 6, 1, 7)
    ]
    for c in send_rows:
        c.start()

    relay_o(1)
    relay_i(1)
    relay_o(2)
    relay_i(2)
    local.wait()
    for c in to_c:
        c.wait_recv()
    for c in send_rows:
        c.wait_recv()

    rows = rows_in[...].reshape(128, 1024)
    up = wts[0].reshape(512, 1024)
    pre = lax.dot_general(rows, up, NT, preferred_element_type=jnp.float32)
    hidden = (0.5 * pre * (1.0 + lax.erf(pre * (2.0**-0.5)))).astype(jnp.bfloat16)
    down = wts[1].reshape(512, 1024)
    total = jnp.dot(hidden, down, preferred_element_type=jnp.float32)
    back_out[...] = total[16:].astype(jnp.bfloat16).reshape(7, 16, 1024)
    send_back = [
        copy(back_out.at[d - 1], back_in.at[d], b_send.at[d], b_recv.at[d], along(8 - d))
        for d in (4, 3, 5, 2, 6, 1, 7)
    ]
    for c in send_back:
        c.start()
    branch = total[:16]
    for c in send_back:
        c.wait_recv()
    for d in range(1, 8):
        branch = branch + back_in[d].astype(jnp.float32)
    out_ref[...] = layer_norm(
        normed.astype(jnp.float32) + branch, g2_ref[...], s2_ref[...]
    ).astype(jnp.bfloat16)
    for c in head + to_o + to_i + to_c + send_rows + send_back:
        c.wait_send()


def layer(*operands):
    dma = pltpu.SemaphoreType.DMA
    vmem = pl.BlockSpec(memory_space=pltpu.VMEM)
    smem = pl.BlockSpec(memory_space=pltpu.SMEM)
    return pl.pallas_call(
        layer_kernel,
        out_shape=jax.ShapeDtypeStruct((16, 1024), jnp.bfloat16),
        in_specs=[vmem] * 5 + [smem] * 2 + [vmem] * 5,
        out_specs=vmem,
        scratch_shapes=[
            pltpu.VMEM((128, 1024), jnp.bfloat16),
            pltpu.VMEM((2, 8, 64, 1024), jnp.bfloat16),
            pltpu.VMEM((8, 16, 1024), jnp.bfloat16),
            pltpu.VMEM((8, 16, 1024), jnp.bfloat16),
            pltpu.VMEM((7, 16, 1024), jnp.bfloat16),
            pltpu.VMEM((8, 16, 1024), jnp.bfloat16),
            dma,
        ]
        + [dma((3,))] * 4
        + [dma((8,))] * 8,
        compiler_params=pltpu.CompilerParams(
            collective_id=0, has_side_effects=True, vmem_limit_bytes=48 * 2**20
        ),
    )(*operands)


def on_device(
    tokens,
    w_qkv,
    w_out,
    k_pages,
    v_pages,
    page_table,
    cache_lens,
    norm1_gain,
    norm1_shift,
    w_up,
    w_down,
    norm2_gain,
    norm2_shift,
):
    return layer(
        tokens,
        w_qkv.reshape(1024, 384),
        w_out,
        k_pages,
        v_pages,
        page_table,
        cache_lens,
        norm1_gain.reshape(1, 1024),
        norm1_shift.reshape(1, 1024),
        jnp.stack([w_up.T, w_down]),
        norm2_gain.reshape(1, 1024),
        norm2_shift.reshape(1, 1024),
    )


def solution(mesh):
    return jax.shard_map(
        on_device,
        mesh=mesh,
        in_specs=(
            P("blk", None),
            P(None, None, "req"),
            P("req", None),
            P("blk", None, "req"),
            P("blk", None, "req"),
            P("blk", None),
            P("blk"),
            P(),
            P(),
            P(None, "blk"),
            P("blk", None),
            P(),
            P(),
        ),
        out_specs=P(("blk", "req"), None),
        check_vma=False,
    )
```

time: 57.6 us -> 48.3 us (0.84)
  local copies, waits for them, and re-layouts: 7.28 us -> 3.99 us
  matrix products: 2.92 us -> 0 us
  other arithmetic: 1.7 us -> 0.03 us
  Pallas kernels: 45.1 us -> 44 us
    dot_general x8 -> x0, matrix products: 2.92 us -> none  [the longest x1 1.02 us: on_device(): partial_out = jnp.dot(attended, w_out, preferred_element_type=jnp.float32)]
    slice x9 -> x0, local copies, waits for them, and re-layouts: 1.43 us -> none  [the longest x3 0.59 us: attend(): key_seq[1:]]
    gather x2 -> x0, local copies, waits for them, and re-layouts: 1.35 us -> none  [the longest x1 0.68 us: attend(): value_pool[page_map].reshape(requests, -1, head_count, head_size)]
    pallas_call x1, Pallas kernels: 45.1 us -> 44 us  [layer(): pl.pallas_call(layer_kernel, out_shape=jax.ShapeDtypeStruct((16, 1024), j...]
    another operation x2 -> x1, other arithmetic: 0.81 us -> 0.03 us  [on_device(): jnp.stack([w_up.T, w_down])]
    unnamed x20 -> x27, local copies, waits for them, and re-layouts: 4.08 us -> 3.63 us
where the time goes in v2:
time: 48.3 us; the launch traced here: 48.2 us
  Pallas kernels  44 us (91%)
  local copies, waits for them, and re-layouts  3.99 us (8%)
    pallas_call x1, Pallas kernels, layer(): pl.pallas_call(layer_kernel, out_shape=jax.ShapeDtypeStruct((16, 1024), j...  44 us
    unnamed x27, local copies, waits for them, and re-layouts  3.63 us

profile of v2, /device:TPU:1, one launch (start us, length us, event | category | flops | bytes accessed | tf_op | source)
XLA Modules:
  0.0 48.2 jit_solution(3767913751009206919)
XLA Ops:
  0.0 0.0 copy-start.10
  0.0 1.4 %copy.16 = bf16[1024,3,128]{0,2,1:T(8,128)(2,1)S(1)} copy(bf16[1024,3,128]{2,0,1:T(8,128)(2,1)} %param.14) | data formatting | bytes 1572864 | tf_op args[1]
  1.4 0.0 copy-start.9
  1.5 0.0 copy-start.11
  1.5 0.0 copy-start
  1.5 0.0 copy-start.1
  1.5 0.0 copy-start.7
  1.5 0.4 copy.17.wqkv_ref
  1.9 0.0 copy-done.10
  1.9 0.5 copy-done.9
  2.4 0.0 copy-start.2
  2.4 0.0 copy-start.3
  2.4 0.0 copy-done.11
  2.4 0.0 copy-start.5
  2.4 0.0 copy-start.6
  2.4 0.1 copy.18.table_ref
  2.5 0.0 copy-start.4
  2.5 0.0 copy-start.8
  2.5 0.1 copy-done
  2.6 0.2 copy-done.1
  2.8 0.0 copy-done.7
  2.8 0.6 %copy-done.2 = bf16[128,1024]{1,0:T(8,128)(2,1)S(1)} copy-done((bf16[128,1024]{1,0:T(8,128)(2,1)S(1)}, bf16[128,1024]{1,0:T(8,128)(2,1)}, u32[]{:S(2)}) %copy-start.2) | copy-done | bytes 262168
  3.4 0.1 copy-done.3
  3.5 0.0 copy-done.5
  3.5 0.0 copy-done.6
  3.5 0.0 copy-done.4
  3.5 0.0 copy-done.8
  3.5 44.0 %shard_map.127 = bf16[16,1024]{1,0:T(8,128)(2,1)S(1)} custom-call(bf16[128,1024]{1,0:T(8,128)(2,1)S(1)} %copy-done.2, bf16[1024,384]{1,0:T(8,128)(2,1)S(1)} %copy.17.wqkv_ref, bf16[128,1024]{1,0:T(8,128)(2,1)S(1)} %copy-done.3, bf16[20,128,128]{2,1,0:T(8,128)(2,1)S(1)} %copy-done, bf16[20,128,128]{2,1,0:T(8,128)(2,1)S(1)} %copy-done.1, ...), custom_call_target="tpu_custom_call" | custom-call | tf_op jit(solution)/shard_map/pallas_call | solution.py:271
  47.5 0.6 %copy.20 = bf16[16,1024]{1,0:T(8,128)(2,1)} copy(bf16[16,1024]{1,0:T(8,128)(2,1)S(1)} %shard_map.127) | data formatting | bytes 65536
  (1 shorter events, 0.0 us)
Async XLA Ops:
  0.0 1.9 %copy-start.10 = (bf16[1024,64]{0,1:T(8,128)(2,1)S(1)}, bf16[1024,64]{0,1:T(8,128)(2,1)}, u32[]{:S(2)}) copy-start(bf16[1024,64]{0,1:T(8,128)(2,1)} %param.22) | copy-start | bytes 393220
  1.4 0.9 %copy-start.9 = (bf16[64,1024]{1,0:T(8,128)(2,1)S(1)}, bf16[64,1024]{1,0:T(8,128)(2,1)}, u32[]{:S(2)}) copy-start(bf16[64,1024]{1,0:T(8,128)(2,1)} %param.23) | copy-start | bytes 393220
  1.5 0.9 %copy-start.11 = (s32[5,4]{0,1:T(4,128)S(1)}, s32[5,4]{0,1:T(4,128)}, u32[]{:S(2)}) copy-start(s32[5,4]{0,1:T(4,128)} %param.18) | copy-start | bytes 244
  1.5 1.2 %copy-start = (bf16[20,128,128]{2,1,0:T(8,128)(2,1)S(1)}, bf16[20,128,128]{2,1,0:T(8,128)(2,1)}, u32[]{:S(2)}) copy-start(bf16[20,128,128]{2,1,0:T(8,128)(2,1)} %k_ref.1) | copy-start | bytes 1966084
  1.5 1.3 %copy-start.1 = (bf16[20,128,128]{2,1,0:T(8,128)(2,1)S(1)}, bf16[20,128,128]{2,1,0:T(8,128)(2,1)}, u32[]{:S(2)}) copy-start(bf16[20,128,128]{2,1,0:T(8,128)(2,1)} %v_ref.1) | copy-start | bytes 1966084
  1.5 1.3 %copy-start.7 = (f32[1024]{0:T(1024)S(1)}, f32[1024]{0:T(1024)}, u32[]{:S(2)}) copy-start(f32[1024]{0:T(1024)} %param.25) | copy-start | bytes 12292
  2.4 1.0 %copy-start.2 = (bf16[128,1024]{1,0:T(8,128)(2,1)S(1)}, bf16[128,1024]{1,0:T(8,128)(2,1)}, u32[]{:S(2)}) copy-start(bf16[128,1024]{1,0:T(8,128)(2,1)} %tok_ref.1) | copy-start | bytes 786436
  2.4 1.1 %copy-start.3 = (bf16[128,1024]{1,0:T(8,128)(2,1)S(1)}, bf16[128,1024]{1,0:T(8,128)(2,1)}, u32[]{:S(2)}) copy-start(bf16[128,1024]{1,0:T(8,128)(2,1)} %wout_ref.1) | copy-start | bytes 786436
  2.4 1.1 %copy-start.5 = (f32[1024]{0:T(1024)S(1)}, f32[1024]{0:T(1024)}, u32[]{:S(2)}) copy-start(f32[1024]{0:T(1024)} %param.21) | copy-start | bytes 12292
  2.4 1.1 %copy-start.6 = (f32[1024]{0:T(1024)S(1)}, f32[1024]{0:T(1024)}, u32[]{:S(2)}) copy-start(f32[1024]{0:T(1024)} %param.24) | copy-start | bytes 12292
  2.5 1.0 %copy-start.4 = (f32[1024]{0:T(1024)S(1)}, f32[1024]{0:T(1024)}, u32[]{:S(2)}) copy-start(f32[1024]{0:T(1024)} %param.20) | copy-start | bytes 12292
  2.5 1.0 %copy-start.8 = (s32[5]{0:T(128)S(1)}, s32[5]{0:T(128)}, u32[]{:S(2)}) copy-start(s32[5]{0:T(128)} %lens_ref.1) | copy-start | bytes 64

commit v3 on v2

v3 whole, which is shorter than its diff:
```python
import jax
import jax.numpy as jnp
from jax import lax
from jax.experimental import pallas as pl
from jax.experimental.pallas import tpu as pltpu
from jax.sharding import PartitionSpec as P

HD = 64
PROMPT = 124
MESH = pl.DeviceIdType.MESH
epsilon = 1e-05
masked_score = -1e30
NT = (((1,), (1,)), ((), ()))


def layer_norm(values, gain_vec, shift_vec):
    center = values - jnp.mean(values, axis=-1, keepdims=True)
    spread = jnp.mean(center * center, axis=-1, keepdims=True)
    return center * lax.rsqrt(spread + epsilon) * gain_vec + shift_vec


def attention(proj, k_ref, v_ref, table_ref, lens_ref):
    query = (proj[:, :128] * 0.125).astype(jnp.bfloat16)
    key_new = proj[:, 128:256]
    value_new = proj[:, 256:]

    def heads(rows):
        low = lax.broadcasted_iota(jnp.int32, rows.shape, 1) < HD
        zero = jnp.zeros_like(rows)
        return jnp.concatenate([jnp.where(low, rows, zero), jnp.where(low, zero, rows)], axis=0)

    def attend(rows, first, keys, values, valid):
        count = rows.shape[0]
        both = heads(rows)
        old = lax.dot_general(both, keys, NT, preferred_element_type=jnp.float32)
        old = jnp.where(valid, old, masked_score)
        new = lax.dot_general(both, key_new, NT, preferred_element_type=jnp.float32)
        token = lax.broadcasted_iota(jnp.int32, new.shape, 0) % count + first
        other = lax.broadcasted_iota(jnp.int32, new.shape, 1)
        seen = (other == token) | ((other < token) & (token < PROMPT))
        new = jnp.where(seen, new, masked_score)
        top = jnp.maximum(jnp.max(old, -1, keepdims=True), jnp.max(new, -1, keepdims=True))
        old = jnp.exp(old - top)
        new = jnp.exp(new - top)
        total = jnp.sum(old, -1, keepdims=True) + jnp.sum(new, -1, keepdims=True)
        mixed = jnp.dot(old.astype(jnp.bfloat16), values, preferred_element_type=jnp.float32)
        mixed = mixed + jnp.dot(
            new.astype(jnp.bfloat16), value_new, preferred_element_type=jnp.float32
        )
        mixed = mixed / total
        low = lax.broadcasted_iota(jnp.int32, (count, 128), 1) < HD
        return jnp.where(low, mixed[:count], mixed[count:])

    def cached(ref, request):
        return [ref[table_ref[p, request]] for p in range(4)]

    column = lax.broadcasted_iota(jnp.int32, (1, 512), 1)
    prompt = attend(
        query,
        0,
        jnp.concatenate(cached(k_ref, 0), axis=0),
        jnp.concatenate(cached(v_ref, 0), axis=0),
        column < lens_ref[0],
    )
    column = lax.broadcasted_iota(jnp.int32, (32, 2048), 1)
    row = lax.broadcasted_iota(jnp.int32, (32, 2048), 0) % 16 - 12
    valid = jnp.zeros((32, 2048), jnp.bool_)
    for i in range(4):
        position = column - 512 * i
        valid = valid | ((row == i) & (position >= 0) & (position < lens_ref[1 + i]) & (position < 512))
    decode = attend(
        query[112:],
        112,
        jnp.concatenate([page for i in range(4) for page in cached(k_ref, 1 + i)], axis=0),
        jnp.concatenate([page for i in range(4) for page in cached(v_ref, 1 + i)], axis=0),
        valid,
    )
    last = lax.broadcasted_iota(jnp.int32, (16, 128), 0) >= 12
    return jnp.concatenate(
        [prompt[:112], jnp.where(last, decode, prompt[112:])], axis=0
    ).astype(jnp.bfloat16)


def layer_kernel(
    tok_ref,
    wqkv_hbm,
    wout_hbm,
    k_hbm,
    v_hbm,
    table_ref,
    lens_ref,
    g1_ref,
    s1_ref,
    up_hbm,
    down_hbm,
    g2_ref,
    s2_ref,
    out_ref,
    wqkv_ref,
    wout_ref,
    k_ref,
    v_ref,
    part_ref,
    wts,
    head_in,
    rows_in,
    back_out,
    back_in,
    local_sem,
    o_send,
    o_recv,
    i_send,
    i_recv,
    c_send,
    c_recv,
    h_send,
    h_recv,
    y_send,
    y_recv,
    b_send,
    b_recv,
):
    blk = lax.axis_index("blk")
    req = lax.axis_index("req")
    y = blk // 8
    k = (blk // 2) % 4
    core = blk % 2
    zlo = req // 4
    x = req % 4
    step = 2 * zlo - 1
    outer = (y * 8 + ((k + step + 4) % 4) * 2 + core, (1 - zlo) * 4 + x)
    inner = (blk, (1 - zlo) * 4 + x)
    sibling = (blk + 1 - 2 * core, req)

    def across(e):
        z = zlo if e < 4 else 1 - zlo
        return (blk, z * 4 + (x + e) % 4)

    def along(d):
        return (((y + d) % 8) * 8 + blk % 8, req)

    def slot(dk):
        return ((k + dk + 8) % 4) * 2 + core

    own = slot(0)
    barrier = pltpu.get_barrier_semaphore()
    for peer in [across(e) for e in range(1, 8)] + [along(d) for d in range(1, 8)] + [outer, sibling]:
        pl.semaphore_signal(barrier, inc=1, device_id=peer, device_id_type=MESH)
    loads = [
        pltpu.make_async_copy(src, dst, local_sem.at[n])
        for n, (src, dst) in enumerate(
            [
                (up_hbm, wts.at[0, own]),
                (down_hbm, wts.at[1, own]),
                (wqkv_hbm, wqkv_ref),
                (k_hbm, k_ref),
                (v_hbm, v_ref),
                (wout_hbm, wout_ref),
            ]
        )
    ]
    for c in loads:
        c.start()

    def copy(src, dst, send, recv, peer):
        return pltpu.make_async_remote_copy(
            src_ref=src,
            dst_ref=dst,
            send_sem=send,
            recv_sem=recv,
            device_id=peer,
            device_id_type=MESH,
        )

    def halves(kind, place):
        return [wts.at[kind, place, pl.ds(32 * h, 32)] for h in range(2)]

    from_o = halves(zlo, slot(step)) + halves(1 - zlo, slot(step)) + halves(zlo, slot(2 * step))
    from_i = halves(1 - zlo, slot(-step)) + halves(zlo, slot(-step)) + halves(1 - zlo, slot(-2 * step))
    mine_o = halves(1 - zlo, own) + halves(zlo, own) + from_i[:2]
    to_o = [copy(c, c, o_send.at[n], o_recv.at[n], outer) for n, c in enumerate(mine_o)]
    to_i = [copy(c, c, i_send.at[n], i_recv.at[n], inner) for n, c in enumerate(from_o)]
    to_c = [
        copy(c, c, c_send.at[n], c_recv.at[n], sibling)
        for n, c in enumerate(from_o + from_i + [wts.at[0, own], wts.at[1, own]])
    ]
    far = (6, 2, 5, 7, 1, 3, 4)
    head = [
        copy(
            part_ref.at[pl.ds(pl.multiple_of(across(e)[1] * 16, 16), 16)],
            head_in.at[e],
            h_send.at[e],
            h_recv.at[e],
            across(e),
        )
        for e in far
    ]

    def relay_o(n):
        to_o[n].wait_recv()
        to_i[n].start()
        to_c[n].start()

    def relay_i(n):
        to_i[n].wait_recv()
        if n < 2:
            to_o[4 + n].start()
        to_c[6 + n].start()

    loads[0].wait()
    loads[1].wait()
    pl.semaphore_wait(barrier, 16)
    for c in to_o[:4] + to_c[12:]:
        c.start()

    loads[2].wait()
    proj = jnp.concatenate(
        [
            jnp.dot(tok_ref[...], wqkv_ref[n], preferred_element_type=jnp.float32).astype(jnp.bfloat16)
            for n in range(3)
        ],
        axis=1,
    )
    loads[3].wait()
    loads[4].wait()
    attended = attention(proj, k_ref, v_ref, table_ref, lens_ref)
    loads[5].wait()
    part_ref[...] = jnp.dot(
        attended, wout_ref[...], preferred_element_type=jnp.float32
    ).astype(jnp.bfloat16)
    for c in head:
        c.start()

    relay_o(0)
    relay_o(1)
    relay_o(2)
    relay_i(0)
    relay_o(3)
    relay_i(1)
    relay_i(2)
    relay_o(4)

    for c in head:
        c.wait_recv()
    mine = pl.ds(pl.multiple_of(req * 16, 16), 16)
    mixed = part_ref[mine].astype(jnp.float32)
    for e in range(1, 8):
        mixed = mixed + head_in[e].astype(jnp.float32)
    normed = layer_norm(
        tok_ref[mine].astype(jnp.float32) + mixed, g1_ref[...], s1_ref[...]
    ).astype(jnp.bfloat16)
    rows_in[0] = normed
    send_rows = {
        d: copy(rows_in.at[0], rows_in.at[d], y_send.at[d], y_recv.at[d], along(d))
        for d in (4, 3, 5, 2, 6, 1, 7)
    }
    for c in send_rows.values():
        c.start()

    relay_i(3)
    relay_o(5)
    relay_i(4)
    relay_i(5)
    for c in to_c:
        c.wait_recv()

    send_back = {}
    for pair in ((4, 0), (3, 5), (2, 6), (1, 7)):
        for d in pair:
            if d:
                send_rows[d].wait_recv()
        rows = jnp.concatenate([rows_in[d] for d in pair], axis=0)
        up = wts[0].reshape(512, 1024)
        pre = lax.dot_general(rows, up, NT, preferred_element_type=jnp.float32)
        hidden = (0.5 * pre * (1.0 + lax.erf(pre * (2.0**-0.5)))).astype(jnp.bfloat16)
        down = wts[1].reshape(512, 1024)
        total = jnp.dot(hidden, down, preferred_element_type=jnp.float32)
        for n, d in enumerate(pair):
            piece = total[16 * n : 16 * n + 16]
            if d == 0:
                branch = piece
            else:
                back_out[d] = piece.astype(jnp.bfloat16)
                send_back[d] = copy(
                    back_out.at[d], back_in.at[d], b_send.at[d], b_recv.at[d], along(8 - d)
                )
                send_back[d].start()
    for d in (4, 3, 5, 2, 6, 1, 7):
        send_back[d].wait_recv()
        branch = branch + back_in[d].astype(jnp.float32)
    out_ref[...] = layer_norm(
        normed.astype(jnp.float32) + branch, g2_ref[...], s2_ref[...]
    ).astype(jnp.bfloat16)
    for c in head + to_o + to_i + to_c + list(send_rows.values()) + list(send_back.values()):
        c.wait_send()


def layer(*operands):
    dma = pltpu.SemaphoreType.DMA
    vmem = pl.BlockSpec(memory_space=pltpu.VMEM)
    smem = pl.BlockSpec(memory_space=pltpu.SMEM)
    hbm = pl.BlockSpec(memory_space=pltpu.HBM)
    half = jnp.bfloat16
    return pl.pallas_call(
        layer_kernel,
        out_shape=jax.ShapeDtypeStruct((16, 1024), half),
        in_specs=[vmem] + [hbm] * 4 + [smem] * 2 + [vmem] * 2 + [hbm] * 2 + [vmem] * 2,
        out_specs=vmem,
        scratch_shapes=[
            pltpu.VMEM((3, 1024, 128), half),
            pltpu.VMEM((128, 1024), half),
            pltpu.VMEM((20, 128, 128), half),
            pltpu.VMEM((20, 128, 128), half),
            pltpu.VMEM((128, 1024), half),
            pltpu.VMEM((2, 8, 64, 1024), half),
            pltpu.VMEM((8, 16, 1024), half),
            pltpu.VMEM((8, 16, 1024), half),
            pltpu.VMEM((8, 16, 1024), half),
            pltpu.VMEM((8, 16, 1024), half),
            dma((6,)),
        ]
        + [dma((6,))] * 4
        + [dma((14,))] * 2
        + [dma((8,))] * 6,
        compiler_params=pltpu.CompilerParams(
            collective_id=0, has_side_effects=True, vmem_limit_bytes=67043328
        ),
    )(*operands)


def on_device(
    tokens,
    w_qkv,
    w_out,
    k_pages,
    v_pages,
    page_table,
    cache_lens,
    norm1_gain,
    norm1_shift,
    w_up,
    w_down,
    norm2_gain,
    norm2_shift,
):
    return layer(
        tokens,
        w_qkv.transpose(1, 0, 2),
        w_out,
        k_pages,
        v_pages,
        page_table.T,
        cache_lens,
        norm1_gain.reshape(1, 1024),
        norm1_shift.reshape(1, 1024),
        w_up.T,
        w_down,
        norm2_gain.reshape(1, 1024),
        norm2_shift.reshape(1, 1024),
    )


def solution(mesh):
    return jax.shard_map(
        on_device,
        mesh=mesh,
        in_specs=(
            P("blk", None),
            P(None, None, "req"),
            P("req", None),
            P("blk", None, "req"),
            P("blk", None, "req"),
            P("blk", None),
            P("blk"),
            P(),
            P(),
            P(None, "blk"),
            P("blk", None),
            P(),
            P(),
        ),
        out_specs=P(("blk", "req"), None),
        check_vma=False,
    )
```

time: 48.3 us -> 44.8 us (0.928)
  local copies, waits for them, and re-layouts: 3.99 us -> 1.38 us
  Pallas kernels: 44 us -> 43.2 us
    unnamed x27 -> x1, local copies, waits for them, and re-layouts: 3.63 us -> 1.38 us
    pallas_call x1, Pallas kernels: 44 us -> 43.2 us  [layer(): pl.pallas_call(layer_kernel, out_shape=jax.ShapeDtypeStruct((16, 1024), h...]
where the time goes in v3:
time: 44.8 us; the launch traced here: 44.6 us
  Pallas kernels  43.2 us (96%)
  local copies, waits for them, and re-layouts  1.38 us (3%)
    pallas_call x1, Pallas kernels, layer(): pl.pallas_call(layer_kernel, out_shape=jax.ShapeDtypeStruct((16, 1024), h...  43.2 us
    unnamed x1, local copies, waits for them, and re-layouts  1.38 us

profile of v3, /device:TPU:1, one launch (start us, length us, event | category | flops | bytes accessed | tf_op | source)
XLA Modules:
  0.0 44.6 jit_solution(3151941683913902700)
XLA Ops:
  0.0 43.2 %shard_map.127 = bf16[16,1024]{1,0:T(8,128)(2,1)} custom-call(bf16[128,1024]{1,0:T(8,128)(2,1)} %tok_ref.1, bf16[3,1024,128]{2,1,0:T(8,128)(2,1)} %bitcast.7, bf16[128,1024]{1,0:T(8,128)(2,1)} %wout_hbm.1, bf16[20,128,128]{2,1,0:T(8,128)(2,1)} %k_hbm.1, bf16[20,128,128]{2,1,0:T(8,128)(2,1)} %v_hbm.1, s32[4,5]{1,0:T(4,128)} %bitcast.13, s32[5]{0:T(128)} %lens_ref.1, ...), custom_call_target="tpu_custom_call" | custom-call | tf_op jit(solution)/shard_map/pallas_call | solution.py:304
  43.2 1.4 %copy.15 = bf16[16,1024]{1,0:T(8,128)(2,1)} copy(bf16[16,1024]{1,0:T(8,128)(2,1)} %shard_map.127) | data formatting | bytes 65536

commit v4 on v3

--- a/solution.py
+++ b/solution.py
@@ -82,20 +82,27 @@
 
 
 def layer_kernel(
-    tok_ref,
+    tok_hbm,
     wqkv_hbm,
     wout_hbm,
     k_hbm,
     v_hbm,
+    table_hbm,
+    lens_hbm,
+    g1_hbm,
+    s1_hbm,
+    up_hbm,
+    down_hbm,
+    g2_hbm,
+    s2_hbm,
+    out_ref,
+    tok_ref,
     table_ref,
     lens_ref,
     g1_ref,
     s1_ref,
-    up_hbm,
-    down_hbm,
     g2_ref,
     s2_ref,
-    out_ref,
     wqkv_ref,
     wout_ref,
     k_ref,
@@ -156,6 +163,13 @@
                 (k_hbm, k_ref),
                 (v_hbm, v_ref),
                 (wout_hbm, wout_ref),
+                (tok_hbm, tok_ref),
+                (table_hbm, table_ref),
+                (lens_hbm, lens_ref),
+                (g1_hbm, g1_ref),
+                (s1_hbm, s1_ref),
+                (g2_hbm, g2_ref),
+                (s2_hbm, s2_ref),
             ]
         )
     ]
@@ -173,11 +187,11 @@
         )
 
     def halves(kind, place):
-        return [wts.at[kind, place, pl.ds(32 * h, 32)] for h in range(2)]
+        return [wts.at[kind, place, pl.ds(16 * h, 16)] for h in range(4)]
 
     from_o = halves(zlo, slot(step)) + halves(1 - zlo, slot(step)) + halves(zlo, slot(2 * step))
     from_i = halves(1 - zlo, slot(-step)) + halves(zlo, slot(-step)) + halves(1 - zlo, slot(-2 * step))
-    mine_o = halves(1 - zlo, own) + halves(zlo, own) + from_i[:2]
+    mine_o = halves(1 - zlo, own) + halves(zlo, own) + from_i[:4]
     to_o = [copy(c, c, o_send.at[n], o_recv.at[n], outer) for n, c in enumerate(mine_o)]
     to_i = [copy(c, c, i_send.at[n], i_recv.at[n], inner) for n, c in enumerate(from_o)]
     to_c = [
@@ -203,17 +217,18 @@
 
     def relay_i(n):
         to_i[n].wait_recv()
-        if n < 2:
-            to_o[4 + n].start()
-        to_c[6 + n].start()
+        if n < 4:
+            to_o[8 + n].start()
+        to_c[12 + n].start()
 
     loads[0].wait()
     loads[1].wait()
     pl.semaphore_wait(barrier, 16)
-    for c in to_o[:4] + to_c[12:]:
+    for c in to_o[:8] + to_c[24:]:
         c.start()
 
     loads[2].wait()
+    loads[6].wait()
     proj = jnp.concatenate(
         [
             jnp.dot(tok_ref[...], wqkv_ref[n], preferred_element_type=jnp.float32).astype(jnp.bfloat16)
@@ -223,8 +238,12 @@
     )
     loads[3].wait()
     loads[4].wait()
+    loads[7].wait()
+    loads[8].wait()
     attended = attention(proj, k_ref, v_ref, table_ref, lens_ref)
     loads[5].wait()
+    for c in loads[9:]:
+        c.wait()
     part_ref[...] = jnp.dot(
         attended, wout_ref[...], preferred_element_type=jnp.float32
     ).astype(jnp.bfloat16)
@@ -234,11 +253,19 @@
     relay_o(0)
     relay_o(1)
     relay_o(2)
+    relay_o(3)
     relay_i(0)
-    relay_o(3)
+    relay_o(4)
     relay_i(1)
+    relay_o(5)
     relay_i(2)
-    relay_o(4)
+    relay_o(6)
+    relay_i(3)
+    relay_o(7)
+    relay_i(4)
+    relay_o(8)
+    relay_i(5)
+    relay_o(9)
 
     for c in head:
         c.wait_recv()
@@ -257,10 +284,15 @@
     for c in send_rows.values():
         c.start()
 
-    relay_i(3)
-    relay_o(5)
-    relay_i(4)
-    relay_i(5)
+    relay_i(6)
+    relay_o(10)
+    relay_i(7)
+    relay_o(11)
+    relay_i(8)
+    relay_i(9)
+    relay_i(10)
+    relay_i(11)
+
     for c in to_c:
         c.wait_recv()
 
@@ -298,15 +330,20 @@
 def layer(*operands):
     dma = pltpu.SemaphoreType.DMA
     vmem = pl.BlockSpec(memory_space=pltpu.VMEM)
-    smem = pl.BlockSpec(memory_space=pltpu.SMEM)
     hbm = pl.BlockSpec(memory_space=pltpu.HBM)
     half = jnp.bfloat16
     return pl.pallas_call(
         layer_kernel,
         out_shape=jax.ShapeDtypeStruct((16, 1024), half),
-        in_specs=[vmem] + [hbm] * 4 + [smem] * 2 + [vmem] * 2 + [hbm] * 2 + [vmem] * 2,
+        in_specs=[hbm] * 13,
         out_specs=vmem,
         scratch_shapes=[
+            pltpu.VMEM((128, 1024), half),
+            pltpu.SMEM((4, 5), jnp.int32),
+            pltpu.SMEM((5,), jnp.int32),
+        ]
+        + [pltpu.VMEM((1, 1024), jnp.float32)] * 4
+        + [
             pltpu.VMEM((3, 1024, 128), half),
             pltpu.VMEM((128, 1024), half),
             pltpu.VMEM((20, 128, 128), half),
@@ -317,10 +354,10 @@
             pltpu.VMEM((8, 16, 1024), half),
             pltpu.VMEM((8, 16, 1024), half),
             pltpu.VMEM((8, 16, 1024), half),
-            dma((6,)),
+            dma((13,)),
         ]
-        + [dma((6,))] * 4
-        + [dma((14,))] * 2
+        + [dma((12,))] * 4
+        + [dma((26,))] * 2
         + [dma((8,))] * 6,
         compiler_params=pltpu.CompilerParams(
             collective_id=0, has_side_effects=True, vmem_limit_bytes=67043328

time: 44.8 us -> 42.6 us (0.951); the launches traced: 44.6 us -> 41.8 us
  Pallas kernels: 43.2 us -> 40.4 us
    pallas_call x1, Pallas kernels: 43.2 us -> 40.4 us  [layer(): pl.pallas_call(layer_kernel, out_shape=jax.ShapeDtypeStruct((16, 1024), h...]
where the time goes in v4:
time: 42.6 us; the launch traced here: 41.8 us
  Pallas kernels  40.4 us (95%)
  local copies, waits for them, and re-layouts  1.38 us (3%)
    pallas_call x1, Pallas kernels, layer(): pl.pallas_call(layer_kernel, out_shape=jax.ShapeDtypeStruct((16, 1024), h...  40.4 us
    unnamed x1, local copies, waits for them, and re-layouts  1.38 us

profile of v4, /device:TPU:1, one launch (start us, length us, event | category | flops | bytes accessed | tf_op | source)
XLA Modules:
  0.0 41.8 jit_solution(5635991772412673135)
XLA Ops:
  0.0 40.4 %shard_map.127 = bf16[16,1024]{1,0:T(8,128)(2,1)} custom-call(bf16[128,1024]{1,0:T(8,128)(2,1)} %tok_hbm.1, bf16[3,1024,128]{2,1,0:T(8,128)(2,1)} %bitcast.7, bf16[128,1024]{1,0:T(8,128)(2,1)} %wout_hbm.1, bf16[20,128,128]{2,1,0:T(8,128)(2,1)} %k_hbm.1, bf16[20,128,128]{2,1,0:T(8,128)(2,1)} %v_hbm.1, s32[4,5]{1,0:T(4,128)} %bitcast.13, s32[5]{0:T(128)} %lens_hbm.1, ...), custom_call_target="tpu_custom_call" | custom-call | tf_op jit(solution)/shard_map/pallas_call | solution.py:335
  40.4 1.4 %copy.15 = bf16[16,1024]{1,0:T(8,128)(2,1)} copy(bf16[16,1024]{1,0:T(8,128)(2,1)} %shard_map.127) | data formatting | bytes 65536

commit v5 on v4

--- a/solution.py
+++ b/solution.py
@@ -297,7 +297,7 @@
         c.wait_recv()
 
     send_back = {}
-    for pair in ((4, 0), (3, 5), (2, 6), (1, 7)):
+    for pair in ((4, 3, 5, 0), (2, 6, 1, 7)):
         for d in pair:
             if d:
                 send_rows[d].wait_recv()

time: 42.6 us -> 42.3 us (level)
  the two profiles are of different devices: /device:TPU:1 before, /device:TPU:65 now
where the time goes in v5:
time: 42.3 us; the launch traced here: 42.1 us
  Pallas kernels  40.7 us (96%)
  local copies, waits for them, and re-layouts  1.38 us (3%)
    pallas_call x1, Pallas kernels, layer(): pl.pallas_call(layer_kernel, out_shape=jax.ShapeDtypeStruct((16, 1024), h...  40.7 us
    unnamed x1, local copies, waits for them, and re-layouts  1.38 us

profile of v5, /device:TPU:65, one launch (start us, length us, event | category | flops | bytes accessed | tf_op | source)
XLA Modules:
  0.0 42.1 jit_solution(5367770619103213858)
XLA Ops:
  0.0 40.7 %shard_map.127 = bf16[16,1024]{1,0:T(8,128)(2,1)} custom-call(bf16[128,1024]{1,0:T(8,128)(2,1)} %tok_hbm.1, bf16[3,1024,128]{2,1,0:T(8,128)(2,1)} %bitcast.7, bf16[128,1024]{1,0:T(8,128)(2,1)} %wout_hbm.1, bf16[20,128,128]{2,1,0:T(8,128)(2,1)} %k_hbm.1, bf16[20,128,128]{2,1,0:T(8,128)(2,1)} %v_hbm.1, s32[4,5]{1,0:T(4,128)} %bitcast.13, s32[5]{0:T(128)} %lens_hbm.1, ...), custom_call_target="tpu_custom_call" | custom-call | tf_op jit(solution)/shard_map/pallas_call | solution.py:335
  40.7 1.4 %copy.15 = bf16[16,1024]{1,0:T(8,128)(2,1)} copy(bf16[16,1024]{1,0:T(8,128)(2,1)} %shard_map.127) | data formatting | bytes 65536
